TPU v7x, 32 devices: a whole 2x2x4 slice. The times are simulated.
32 devices in a mesh: seq: 4 (over y, x), res: 8 (over z, core).
Axes of the slice: x: 2, y: 2, z: 4, core: 2. Of those that a mesh axis runs over, the one named last changes fastest.
Arguments:
- alignment: float32 [256, 64, 256], P('seq', 'res'), may hold values from -100 to 100
- pair_features: float32 [64, 64, 128], P('seq', 'res'), may hold values from -100 to 100
- outer_gain: float32 [256], replicated, may hold values from 0.5 to 1.5
- w_outer_in: float32 [256, 64], replicated, may hold values from -0.375 to 0.375
- w_outer_out: float32 [1024, 128], replicated, may hold values from -0.1875 to 0.1875
- pair_gain: float32 [128], replicated, may hold values from 0.5 to 1.5
- w_bias: float32 [128, 8], replicated, may hold values from -30 to 30
- row_gain: float32 [256], replicated, may hold values from 0.5 to 1.5
- w_project: float32 [256, 1024], replicated, may hold values from -0.375 to 0.375
- w_output: float32 [256, 256], replicated, may hold values from -0.375 to 0.375
Outputs:
- alignment_out: float32 [256, 64, 256], P('seq', 'res')
- updated_pair_array: float32 [64, 64, 128], P('seq', 'res')
All inputs are finite; a program needn't handle non-finite values.
Results may differ from a plain program's by a relative error of at most 0.00018.
Values sent between devices are 32-bit elements; how exact they have to be, the bound alone decides.
A program may use at most 128 MiB of HBM per device.

v0:
```python
import jax
import jax.numpy as jnp
from jax import lax
from jax.sharding import PartitionSpec as P

precise = lax.Precision.HIGHEST


def layer_norm(values, scales):
    average = jnp.mean(values, axis=-1, keepdims=True)
    centered = values - average
    variance = jnp.mean(centered * centered, axis=-1, keepdims=True)
    return centered * lax.rsqrt(variance + 1e-05) * scales


def row_attention(sequence, bias_all, row_gain, w_project, w_output):
    residues, channels = sequence.shape
    head_count = bias_all.shape[0]
    head_size = channels // head_count
    normed_rows = layer_norm(sequence, row_gain)
    projected = jnp.dot(
        normed_rows, w_project, precision=precise, preferred_element_type=jnp.float32
    )
    query_map = projected[:, :channels].reshape(residues, head_count, head_size) * head_size ** (
        -0.5
    )
    key_map = projected[:, channels : 2 * channels].reshape(residues, head_count, head_size)
    value_map = projected[:, 2 * channels : 3 * channels].reshape(residues, head_count, head_size)
    gate_map = projected[:, 3 * channels :]
    scores = jnp.einsum("ihd,jhd->hij", query_map, key_map, precision=precise) + bias_all
    weights = jax.nn.softmax(scores, axis=-1)
    mixed_heads = jnp.einsum("hij,jhd->ihd", weights, value_map, precision=precise).reshape(
        residues, channels
    )
    gated_out = jax.nn.sigmoid(gate_map) * mixed_heads
    return sequence + jnp.dot(
        gated_out, w_output, precision=precise, preferred_element_type=jnp.float32
    )


def on_device(
    alignment,
    pair_features,
    outer_gain,
    w_outer_in,
    w_outer_out,
    pair_gain,
    w_bias,
    row_gain,
    w_project,
    w_output,
):
    sequence_local_count, residue_local_count, alignment_channel_count = alignment.shape
    row_block = pair_features.shape[0]
    sequence_group_list = lax.axis_size("res")
    seq_groups = lax.axis_size("seq")
    seq_total = sequence_local_count * seq_groups
    channels = w_outer_in.shape[1] // 2
    normed_rows = layer_norm(alignment, outer_gain)
    both_maps = jnp.einsum("src,cd->sdr", normed_rows, w_outer_in, precision=precise)
    left_maps = both_maps[:, :channels]
    right_maps = both_maps[:, channels:]
    left_all = lax.all_gather(left_maps, "res", axis=2, tiled=True)
    left_rows = lax.all_to_all(left_all, "seq", split_axis=2, concat_axis=0, tiled=True)
    product = jnp.einsum(
        "sxi,syj->ijxy",
        left_rows,
        lax.all_gather(right_maps, "seq", axis=0, tiled=True),
        precision=precise,
    )
    summed = product.reshape(row_block, residue_local_count, channels * channels)
    pair_update = jnp.einsum("ijk,kc->ijc", summed / seq_total, w_outer_out, precision=precise)
    updated_pair_array = pair_features + pair_update
    bias_tile = jnp.einsum(
        "ijc,ch->hij", layer_norm(updated_pair_array, pair_gain), w_bias, precision=precise
    )
    bias_rows = lax.all_gather(bias_tile, "res", axis=2, tiled=True)
    bias_all = lax.all_gather(bias_rows, "seq", axis=1, tiled=True)
    sequence_grouped_rows = alignment.reshape(
        sequence_group_list,
        sequence_local_count // sequence_group_list,
        residue_local_count,
        alignment_channel_count,
    )
    sequences = lax.all_to_all(
        sequence_grouped_rows, "res", split_axis=0, concat_axis=2, tiled=True
    )[0]
    updated = jax.vmap(row_attention, in_axes=(0, None, None, None, None))(
        sequences, bias_all, row_gain, w_project, w_output
    )
    attended = updated[None]
    returned_result = lax.all_to_all(attended, "res", split_axis=2, concat_axis=0, tiled=True)
    return (
        returned_result.reshape(sequence_local_count, residue_local_count, alignment_channel_count),
        updated_pair_array,
    )


def solution(mesh):
    in_specs = (
        P("seq", "res", None),
        P("seq", "res", None),
        P(),
        P(),
        P(),
        P(),
        P(),
        P(),
        P(),
        P(),
    )
    out_specs = (P("seq", "res", None), P("seq", "res", None))
    return jax.shard_map(
        on_device, mesh=mesh, in_specs=in_specs, out_specs=out_specs, check_vma=False
    )
```

profile of v0, /device:TPU:0, one launch (start us, length us, event | category | flops | bytes accessed | tf_op | source)
XLA Modules:
  0.0 148.9 jit_solution(3641051938862273192)
XLA Ops:
  0.6 1.3 reduce_sum.65
  1.9 1.3 multiply_reduce_fusion
  3.2 1.7 %convolution_bitcast_fusion = f32[64,64,8]{1,2,0:T(8,128)S(1)} fusion(f32[64,8,256]{2,1,0:T(8,128)} %param.10, f32[256]{0:T(256)} %param.12, f32[64,8]{1,0:T(8,128)S(1)} %add_rsqrt_fusion, f32[64,8]{1,0:T(8,128)S(1)} %broadcast_multiply_fusion, f32[256,64]{0,1:T(8,128)} %param.13), kind=kOutput, calls=%fused_computation.8 | convolution fusion | flops 101056512 | bytes 726016 | tf_op jit(solution)/shard_map/src,cd->sdr/dot_general | solution.py:60
  5.1 25.1 %all_gather.13 = f32[64,32,64]{1,2,0:T(8,128)S(1)} all-gather(f32[64,32,8]{1,2,0:T(8,128)S(1)} %get-tuple-element.5), channel_id=1, replica_groups=mesh['seq'=4,'res'=8] {'res'}, dimensions={2}, use_global_device_ids=true | all-gather | bytes 589824 | tf_op jit(solution)/shard_map/all_gather | solution.py:63
  30.2 2.1 %copy.39 = f32[64,32,64]{0,1,2:T(8,128)} copy(f32[64,32,64]{1,2,0:T(8,128)S(1)} %all_gather.13) | data formatting | bytes 1048576 | tf_op jit(solution)/shard_map/all_gather | solution.py:63
  32.3 2.7 %reshape.99 = f32[4,1,32768]{2,1,0:T(1,128)} reshape(f32[64,32,64]{2,1,0:T(8,128)} %bitcast.73) | data formatting | bytes 1048576
  35.0 3.7 %all-to-all-start.1 = ((f32[4,1,32768]{2,1,0:T(1,128)}), f32[4,1,32768]{2,1,0:T(1,128)S(1)}, u32[]{:S(2)}, u32[]{:S(2)}) async-start(f32[4,1,32768]{2,1,0:T(1,128)} %reshape.99), calls=%async_computation.1 | async-start | bytes 1048576 | tf_op jit(solution)/shard_map/all_to_all | solution.py:64
  38.7 18.5 %all_gather.12 = f32[256,32,8]{1,2,0:T(8,128)S(1)} all-gather(f32[64,32,8]{1,2,0:T(8,128)S(1)} %get-tuple-element.6), channel_id=1, replica_groups=mesh['seq'=4,'res'=8] {'seq'}, dimensions={0}, use_global_device_ids=true | all-gather | bytes 327680 | tf_op jit(solution)/shard_map/all_gather | solution.py:68
  57.6 4.3 %all-to-all-start = ((f32[8,8,8,256]{3,2,1,0:T(8,128)}), f32[8,8,8,256]{3,2,1,0:T(8,128)}, u32[]{:S(2)}, u32[]{:S(2)}) async-start(f32[8,8,8,256]{3,2,1,0:T(8,128)} %bitcast), calls=%async_computation | async-start | bytes 1048576 | tf_op jit(solution)/shard_map/all_to_all | solution.py:85
  62.5 2.1 %reduce.2 = f32[4,32768]{1,0:T(4,128)S(1)} reduce(f32[4,1,32768]{2,1,0:T(1,128)S(1)} %all-to-all-done.1, f32[]{:T(128)} %broadcast.97), dimensions={1}, to_apply=%all_to_all.38.reduce_sub_computation | reduce | bytes 1048580 | tf_op jit(solution)/shard_map/all_to_all | solution.py:64
  65.2 0.7 copy.59
  65.9 0.6 reshape.94
  66.5 3.2 %multiply_bitcast_fusion = f32[16,8,32,32]{2,1,0,3:T(8,128)} fusion(f32[256,32,8,1]{0,2,3,1:T(8,128)S(1)} %copy.49, f32[256,32,16,1]{0,1,2,3:T(8,128)S(1)} %reshape.94), kind=kOutput, calls=%fused_computation.3 | convolution fusion | flops 402784256 | bytes 1310720 | tf_op jit(solution)/shard_map/sxi,syj->ijxy/dot_general | solution.py:65
  69.7 2.3 %copy.42 = f32[16,8,32,32]{3,2,1,0:T(8,128)S(1)} copy(f32[16,8,32,32]{2,1,0,3:T(8,128)} %multiply_bitcast_fusion) | data formatting | bytes 1048576 | tf_op jit(solution)/shard_map/div | solution.py:72
  72.0 1.7 %div.50 = f32[16,8,1024]{2,1,0:T(8,128)} reshape(f32[16,8,32,32]{3,2,1,0:T(8,128)S(1)} %copy.42) | data formatting | bytes 1048576 | tf_op jit(solution)/shard_map/div | solution.py:72
  73.7 1.9 %fusion.41 = (f32[16,8]{1,0:T(8,128)S(1)}, f32[16,8,128]{2,1,0:T(8,128)S(1)}) fusion(f32[16,8,128]{2,1,0:T(8,128)S(1)} %copy-done.3, f32[16,8,1024]{2,1,0:T(8,128)} %div.50, f32[1024,128]{1,0:T(8,128)} %param.14), kind=kOutput, calls=%fused_computation.60 | convolution fusion | flops 201359232 | bytes 1180160 | tf_op jit(solution)/shard_map/ijk,kc->ijc/dot_general | solution.py:72
  76.1 14.9 %all_gather.14 = f32[8,16,64]{0,2,1:T(8,128)S(1)} all-gather(f32[8,16,8]{0,2,1:T(8,128)S(1)} %convolution_bitcast_fusion.1), channel_id=1, replica_groups=mesh['seq'=4,'res'=8] {'res'}, dimensions={2}, use_global_device_ids=true | all-gather | bytes 36864 | tf_op jit(solution)/shard_map/all_gather | solution.py:77
  91.2 8.4 %all_gather.15 = f32[8,64,64]{2,0,1:T(8,128)S(1)} all-gather(f32[8,16,64]{2,0,1:T(8,128)S(1)} %copy.43), channel_id=1, replica_groups=mesh['seq'=4,'res'=8] {'seq'}, dimensions={1}, use_global_device_ids=true | all-gather | bytes 163840 | tf_op jit(solution)/shard_map/all_gather | solution.py:78
  99.8 1.2 bitcast_reduce_fusion
  101.1 1.3 multiply_reduce_fusion.1
  102.5 2.9 %fusion.4 = f32[8,64,1024]{2,1,0:T(8,128)S(1)} fusion(f32[256,1024]{1,0:T(8,128)S(1)} %copy-done, f32[256]{0:T(256)S(1)} %copy-done.4, f32[8,64]{1,0:T(8,128)S(1)} %rsqrt.28, f32[8,64]{1,0:T(8,128)S(1)} %div.42, f32[8,8,8,256]{3,2,1,0:T(8,128)} %all-to-all-done), kind=kOutput, calls=%fused_computation.11 | convolution fusion | flops 1611005952 | bytes 3675136 | tf_op jit(solution)/shard_map/vmap()/dot_general | solution.py:21
  105.5 1.2 fusion.39
  106.7 2.4 %copy.38 = f32[8,64,256]{1,2,0:T(8,128)} copy(f32[8,64,256]{2,1,0:T(8,128)} %get-tuple-element.2) | data formatting | bytes 1048576 | tf_op jit(solution)/shard_map/vmap()/slice | solution.py:27
  109.1 2.4 %copy.37 = f32[8,64,256]{1,2,0:T(8,128)} copy(f32[8,64,256]{2,1,0:T(8,128)} %get-tuple-element.3) | data formatting | bytes 1048576 | tf_op jit(solution)/shard_map/vmap()/mul | solution.py:24
  111.5 2.4 %copy.36 = f32[8,64,256]{1,2,0:T(8,128)} copy(f32[8,64,256]{2,1,0:T(8,128)} %get-tuple-element.4) | data formatting | bytes 1048576 | tf_op jit(solution)/shard_map/vmap()/slice | solution.py:28
  113.8 5.1 %add_reduce_fusion = (f32[8,8,64]{2,1,0:T(8,128)S(1)}, f32[8,8,64,64]{2,3,1,0:T(8,128)S(1)}) fusion(f32[8,64,64]{1,2,0:T(8,128)S(1)} %copy.44, f32[8,64,8,32]{1,3,2,0:T(8,128)} %bitcast.72, f32[8,64,8,32]{1,3,2,0:T(8,128)} %bitcast.71), kind=kOutput, calls=%fused_computation.4 | convolution fusion | flops 101183488 | bytes 2244608 | tf_op jit(solution)/shard_map/vmap(ihd,jhd->hij)/dot_general | solution.py:30
  119.5 0.7 copy-done.1
  120.2 3.3 %fusion = f32[8,8,32,64]{3,2,1,0:T(8,128)} fusion(f32[8,64,8,32]{1,3,2,0:T(8,128)S(1)} %bitcast.78, f32[8,8,64,64]{2,3,1,0:T(8,128)S(1)} %get-tuple-element.10, f32[8,8,64]{2,1,0:T(8,128)S(1)} %fusion.2, f32[8,8,64]{2,1,0:T(8,128)S(1)} %get-tuple-element.9, f32[8,64,64]{1,2,0:T(8,128)S(1)} %copy.44), kind=kOutput, calls=%fused_computation | convolution fusion | flops 101449728 | bytes 2260992 | tf_op jit(solution)/shard_map/vmap(hij,jhd->ihd)/dot_general | solution.py:32
  123.5 2.3 %copy.46 = f32[8,64,256]{2,1,0:T(8,128)} copy(f32[8,64,256]{1,2,0:T(8,128)} %bitcast.79) | data formatting | bytes 1048576 | tf_op jit(solution)/shard_map/vmap()/reshape | solution.py:32
  125.8 1.9 %fusion.3 = f32[1,8,64,256]{3,2,1,0:T(8,128)S(1)} fusion(f32[8,64,256]{2,1,0:T(8,128)} %copy.46, f32[8,64,1024]{2,1,0:T(8,128)S(1)} %fusion.4, f32[256,256]{1,0:T(8,128)} %param.19, f32[8,8,8,256]{3,2,1,0:T(8,128)} %all-to-all-done), kind=kOutput, calls=%fused_computation.7 | convolution fusion | flops 403308544 | bytes 2359296 | tf_op jit(solution)/shard_map/vmap()/dot_general | solution.py:36
  128.1 19.8 %all_to_all.48 = f32[1,8,64,256]{3,1,0,2:T(8,128)S(1)} all-to-all(f32[1,8,64,256]{3,1,0,2:T(8,128)S(1)} %copy.47), channel_id=1, replica_groups=mesh['seq'=4,'res'=8] {'res'}, dimensions={2} | all-to-all | bytes 1048576 | tf_op jit(solution)/shard_map/all_to_all | solution.py:92
  148.0 1.0 copy.48
  (35 shorter events, 3.4 us)
Async XLA Ops:
  0.6 101.9 %copy-start = (f32[256,1024]{1,0:T(8,128)S(1)}, f32[256,1024]{1,0:T(8,128)}, u32[]{:S(2)}) copy-start(f32[256,1024]{1,0:T(8,128)} %param.18) | copy-start | bytes 3145732
  35.0 22.6 %all-to-all-start.1 = ((f32[4,1,32768]{2,1,0:T(1,128)}), f32[4,1,32768]{2,1,0:T(1,128)S(1)}, u32[]{:S(2)}, u32[]{:S(2)}) async-start(f32[4,1,32768]{2,1,0:T(1,128)} %reshape.99), calls=%async_computation.1 | async-start | bytes 1048576 | tf_op jit(solution)/shard_map/all_to_all | solution.py:64
  57.6 42.2 %all-to-all-start = ((f32[8,8,8,256]{3,2,1,0:T(8,128)}), f32[8,8,8,256]{3,2,1,0:T(8,128)}, u32[]{:S(2)}, u32[]{:S(2)}) async-start(f32[8,8,8,256]{3,2,1,0:T(8,128)} %bitcast), calls=%async_computation | async-start | bytes 1048576 | tf_op jit(solution)/shard_map/all_to_all | solution.py:85
  71.9 1.8 %copy-start.3 = (f32[16,8,128]{2,1,0:T(8,128)S(1)}, f32[16,8,128]{2,1,0:T(8,128)}, u32[]{:S(2)}) copy-start(f32[16,8,128]{2,1,0:T(8,128)} %param.11) | copy-start | bytes 196612
  71.9 3.9 %copy-start.5 = (f32[128,8]{0,1:T(8,128)S(1)}, f32[128,8]{0,1:T(8,128)}, u32[]{:S(2)}) copy-start(f32[128,8]{0,1:T(8,128)} %param.16) | copy-start | bytes 12292
  71.9 3.9 %copy-start.6 = (f32[128]{0:T(128)S(1)}, f32[128]{0:T(128)}, u32[]{:S(2)}) copy-start(f32[128]{0:T(128)} %param.15) | copy-start | bytes 1540
  75.6 29.8 %copy-start.2 = (f32[16,8,128]{2,1,0:T(8,128)}, f32[16,8,128]{2,1,0:T(8,128)S(1)}, u32[]{:S(2)}) copy-start(f32[16,8,128]{2,1,0:T(8,128)S(1)} %get-tuple-element.8) | copy-start | bytes 196612
  75.6 26.9 %copy-start.4 = (f32[256]{0:T(256)S(1)}, f32[256]{0:T(256)}, u32[]{:S(2)}) copy-start(f32[256]{0:T(256)} %param.17) | copy-start | bytes 3076
  118.9 1.2 copy-start.1
where the time goes:
time: 150 us; the launch traced here: 149 us
  blocking collectives  86.8 us (58%)
  local copies, waits for them, and re-layouts  23.6 us (16%)
  matrix products  20.3 us (14%)
  other arithmetic  9.14 us (6%)
  starting transfers between devices  8.05 us (5%)
    all_gather x1, blocking collectives, on_device(): left_all = lax.all_gather(left_maps, 'res', axis=2, tiled=True)  25.1 us
    all_to_all x1, blocking collectives, on_device(): lax.all_to_all(attended, 'res', split_axis=2, concat_axis=0, tiled=True)  19.8 us
    all_gather x1, blocking collectives, on_device(): lax.all_gather(right_maps, 'seq', axis=0, tiled=True)  18.5 us
    all_gather x1, blocking collectives, on_device(): bias_rows = lax.all_gather(bias_tile, 'res', axis=2, tiled=True)  14.9 us
    all_gather x1, blocking collectives, on_device(): bias_all = lax.all_gather(bias_rows, 'seq', axis=1, tiled=True)  8.4 us
    dot_general x1, matrix products, row_attention(): jnp.einsum('ihd,jhd->hij', query_map, key_map, precision=precise) + bias_all  5.09 us
    all_to_all x1, starting transfers between devices, on_device(): lax.all_to_all(sequence_grouped_rows, 'res', split_axis=0, concat_axis=2,...  4.34 us
    div x2, local copies, waits for them, and re-layouts, on_device(): summed / seq_total  4 us
  transfers between devices with their start and end apart: 2, of which 0 were waited for; matrix products, arithmetic and copies ran while one was open for 10% of the time, Pallas kernels for 0%

commit v1 on v0

--- a/solution.py
+++ b/solution.py
@@ -1,9 +1,27 @@
+import functools
 import jax
 import jax.numpy as jnp
 from jax import lax
 from jax.sharding import PartitionSpec as P
 
 precise = lax.Precision.HIGHEST
+
+
+def show_side(inputs, join_dim):
+    axis_len = lax.axis_size("res")
+    z2 = sorted(((h, (h + 1) % axis_len) for h in range(axis_len)))
+    s_next = inputs
+    history = [s_next]
+    for k0 in [*range(1, axis_len)]:
+        s_next = lax.ppermute(s_next, "res", z2)
+        history.insert(0, s_next)
+    inter = jnp.concatenate(history, join_dim)
+    main = lax.axis_index("res")
+    y2 = jnp.roll(inter, (main + 1) * inputs.shape[join_dim], join_dim)
+    return y2
+
+
+quarters_name = functools.partial(show_side, join_dim=2)
 
 
 def layer_norm(values, scales):
@@ -74,7 +92,7 @@
     bias_tile = jnp.einsum(
         "ijc,ch->hij", layer_norm(updated_pair_array, pair_gain), w_bias, precision=precise
     )
-    bias_rows = lax.all_gather(bias_tile, "res", axis=2, tiled=True)
+    bias_rows = quarters_name(bias_tile)
     bias_all = lax.all_gather(bias_rows, "seq", axis=1, tiled=True)
     sequence_grouped_rows = alignment.reshape(
         sequence_group_list,

time: 150 us -> 172 us (1.15)
  waiting for transfers between devices: 0.01 us -> 38.2 us
  blocking collectives: 86.8 us -> 69.8 us
    ppermute x0 -> x7, waiting for transfers between devices: none -> 38.2 us  [show_side(): s_next = lax.ppermute(s_next, 'res', z2)]
    all_gather x1 -> x0, blocking collectives: 14.9 us -> none  [on_device(): bias_rows = lax.all_gather(bias_tile, 'res', axis=2, tiled=True)]
    all_to_all x1, blocking collectives: 19.8 us -> 17.7 us  [on_device(): lax.all_to_all(attended, 'res', split_axis=2, concat_axis=0, tiled=True)]
  transfers between devices with their start and end apart: 2 -> 9, of which waited for: 0 -> 7; matrix products, arithmetic and copies ran while one was open for 10% -> 9% of each run, Pallas kernels for 0% -> 0%
where the time goes in v1:
time: 172 us; the launch traced here: 171 us
  blocking collectives  69.8 us (41%)
  waiting for transfers between devices  38.2 us (22%)
  local copies, waits for them, and re-layouts  23.9 us (14%)
  matrix products  21.1 us (12%)
  other arithmetic  9.14 us (5%)
  starting transfers between devices  8.29 us (5%)
    ppermute x7, waiting for transfers between devices, show_side(): s_next = lax.ppermute(s_next, 'res', z2)  38.2 us
    all_gather x1, blocking collectives, on_device(): left_all = lax.all_gather(left_maps, 'res', axis=2, tiled=True)  25.1 us
    all_gather x1, blocking collectives, on_device(): lax.all_gather(right_maps, 'seq', axis=0, tiled=True)  18.5 us
    all_to_all x1, blocking collectives, on_device(): lax.all_to_all(attended, 'res', split_axis=2, concat_axis=0, tiled=True)  17.7 us
    all_gather x1, blocking collectives, on_device(): bias_all = lax.all_gather(bias_rows, 'seq', axis=1, tiled=True)  8.39 us
    dot_general x1, matrix products, row_attention(): jnp.einsum('ihd,jhd->hij', query_map, key_map, precision=precise) + bias_all  5.09 us
    all_to_all x1, starting transfers between devices, on_device(): lax.all_to_all(sequence_grouped_rows, 'res', split_axis=0, concat_axis=2,...  4.34 us
    div x2, local copies, waits for them, and re-layouts, on_device(): summed / seq_total  4 us
  transfers between devices with their start and end apart: 9, of which 7 were waited for; matrix products, arithmetic and copies ran while one was open for 9% of the time, Pallas kernels for 0%

profile of v1, /device:TPU:0, one launch (start us, length us, event | category | flops | bytes accessed | tf_op | source)
XLA Modules:
  0.0 171.3 jit_solution(6462826501815504274)
XLA Ops:
  0.6 1.3 reduce_sum.65
  1.9 1.3 multiply_reduce_fusion
  3.2 1.7 convolution_bitcast_fusion
  5.1 25.1 %all_gather.10 = f32[64,32,64]{1,2,0:T(8,128)S(1)} all-gather(f32[64,32,8]{1,2,0:T(8,128)S(1)} %get-tuple-element.5), channel_id=1, replica_groups=mesh['seq'=4,'res'=8] {'res'}, dimensions={2}, use_global_device_ids=true | all-gather | bytes 589824 | tf_op jit(solution)/shard_map/all_gather | solution.py:81
  30.2 2.1 %copy.39 = f32[64,32,64]{0,1,2:T(8,128)} copy(f32[64,32,64]{1,2,0:T(8,128)S(1)} %all_gather.10) | data formatting | bytes 1048576 | tf_op jit(solution)/shard_map/all_gather | solution.py:81
  32.3 2.7 %reshape.99 = f32[4,1,32768]{2,1,0:T(1,128)} reshape(f32[64,32,64]{2,1,0:T(8,128)} %bitcast.73) | data formatting | bytes 1048576
  35.0 3.7 %all-to-all-start.1 = ((f32[4,1,32768]{2,1,0:T(1,128)}), f32[4,1,32768]{2,1,0:T(1,128)S(1)}, u32[]{:S(2)}, u32[]{:S(2)}) async-start(f32[4,1,32768]{2,1,0:T(1,128)} %reshape.99), calls=%async_computation.1 | async-start | bytes 1048576 | tf_op jit(solution)/shard_map/all_to_all | solution.py:82
  38.7 18.5 %all_gather.9 = f32[256,32,8]{1,2,0:T(8,128)S(1)} all-gather(f32[64,32,8]{1,2,0:T(8,128)S(1)} %get-tuple-element.6), channel_id=1, replica_groups=mesh['seq'=4,'res'=8] {'seq'}, dimensions={0}, use_global_device_ids=true | all-gather | bytes 327680 | tf_op jit(solution)/shard_map/all_gather | solution.py:86
  57.6 4.3 %all-to-all-start = ((f32[8,8,8,256]{3,2,1,0:T(8,128)}), f32[8,8,8,256]{3,2,1,0:T(8,128)}, u32[]{:S(2)}, u32[]{:S(2)}) async-start(f32[8,8,8,256]{3,2,1,0:T(8,128)} %bitcast), calls=%async_computation | async-start | bytes 1048576 | tf_op jit(solution)/shard_map/all_to_all | solution.py:103
  62.5 2.1 %reduce.2 = f32[4,32768]{1,0:T(4,128)S(1)} reduce(f32[4,1,32768]{2,1,0:T(1,128)S(1)} %all-to-all-done.1, f32[]{:T(128)} %broadcast.98), dimensions={1}, to_apply=%all_to_all.38.reduce_sub_computation | reduce | bytes 1048580 | tf_op jit(solution)/shard_map/all_to_all | solution.py:82
  66.5 3.2 %multiply_bitcast_fusion = f32[16,8,32,32]{2,1,0,3:T(8,128)} fusion(f32[256,32,8,1]{0,2,3,1:T(8,128)S(1)} %copy.48, f32[256,32,16,1]{0,1,2,3:T(8,128)S(1)} %reshape.94), kind=kOutput, calls=%fused_computation.3 | convolution fusion | flops 402784256 | bytes 1310720 | tf_op jit(solution)/shard_map/sxi,syj->ijxy/dot_general | solution.py:83
  69.7 2.3 %copy.42 = f32[16,8,32,32]{3,2,1,0:T(8,128)S(1)} copy(f32[16,8,32,32]{2,1,0,3:T(8,128)} %multiply_bitcast_fusion) | data formatting | bytes 1048576 | tf_op jit(solution)/shard_map/div | solution.py:90
  72.0 1.7 %div.50 = f32[16,8,1024]{2,1,0:T(8,128)} reshape(f32[16,8,32,32]{3,2,1,0:T(8,128)S(1)} %copy.42) | data formatting | bytes 1048576 | tf_op jit(solution)/shard_map/div | solution.py:90
  73.7 1.9 %fusion.41 = (f32[16,8]{1,0:T(8,128)S(1)}, f32[16,8,128]{2,1,0:T(8,128)S(1)}) fusion(f32[16,8,128]{2,1,0:T(8,128)S(1)} %copy-done.3, f32[16,8,1024]{2,1,0:T(8,128)} %div.50, f32[1024,128]{1,0:T(8,128)} %param.14), kind=kOutput, calls=%fused_computation.61 | convolution fusion | flops 201359232 | bytes 1180160 | tf_op jit(solution)/shard_map/ijk,kc->ijc/dot_general | solution.py:90
  77.1 5.3 %collective-permute-done = f32[8,16,8]{2,0,1:T(8,128)S(1)} collective-permute-done((f32[8,16,8]{2,0,1:T(8,128)S(1)}, f32[8,16,8]{2,0,1:T(8,128)S(1)}, u32[]{:S(2)}, u32[]{:S(2)}) %collective-permute-start) | collective-permute-done | bytes 4128 | tf_op jit(solution)/shard_map/ppermute | solution.py:16
  82.4 5.5 %collective-permute-done.1 = f32[8,16,8]{2,0,1:T(8,128)S(1)} collective-permute-done((f32[8,16,8]{2,0,1:T(8,128)S(1)}, f32[8,16,8]{2,0,1:T(8,128)S(1)}, u32[]{:S(2)}, u32[]{:S(2)}) %collective-permute-start.1) | collective-permute-done | bytes 4128 | tf_op jit(solution)/shard_map/ppermute | solution.py:16
  87.9 5.5 %collective-permute-done.2 = f32[8,16,8]{2,0,1:T(8,128)S(1)} collective-permute-done((f32[8,16,8]{2,0,1:T(8,128)S(1)}, f32[8,16,8]{2,0,1:T(8,128)S(1)}, u32[]{:S(2)}, u32[]{:S(2)}) %collective-permute-start.2) | collective-permute-done | bytes 4128 | tf_op jit(solution)/shard_map/ppermute | solution.py:16
  93.4 5.5 %collective-permute-done.3 = f32[8,16,8]{2,0,1:T(8,128)S(1)} collective-permute-done((f32[8,16,8]{2,0,1:T(8,128)S(1)}, f32[8,16,8]{2,0,1:T(8,128)S(1)}, u32[]{:S(2)}, u32[]{:S(2)}) %collective-permute-start.3) | collective-permute-done | bytes 4128 | tf_op jit(solution)/shard_map/ppermute | solution.py:16
  98.9 5.5 %collective-permute-done.4 = f32[8,16,8]{2,0,1:T(8,128)S(1)} collective-permute-done((f32[8,16,8]{2,0,1:T(8,128)S(1)}, f32[8,16,8]{2,0,1:T(8,128)S(1)}, u32[]{:S(2)}, u32[]{:S(2)}) %collective-permute-start.4) | collective-permute-done | bytes 4128 | tf_op jit(solution)/shard_map/ppermute | solution.py:16
  104.4 5.5 %collective-permute-done.5 = f32[8,16,8]{2,0,1:T(8,128)S(1)} collective-permute-done((f32[8,16,8]{2,0,1:T(8,128)S(1)}, f32[8,16,8]{2,0,1:T(8,128)S(1)}, u32[]{:S(2)}, u32[]{:S(2)}) %collective-permute-start.5) | collective-permute-done | bytes 4128 | tf_op jit(solution)/shard_map/ppermute | solution.py:16
  109.9 5.5 %collective-permute-done.6 = f32[8,16,8]{2,0,1:T(8,128)S(1)} collective-permute-done((f32[8,16,8]{2,0,1:T(8,128)S(1)}, f32[8,16,8]{2,0,1:T(8,128)S(1)}, u32[]{:S(2)}, u32[]{:S(2)}) %collective-permute-start.6) | collective-permute-done | bytes 4128 | tf_op jit(solution)/shard_map/ppermute | solution.py:16
  115.8 8.4 %all_gather.11 = f32[8,64,64]{2,0,1:T(8,128)S(1)} all-gather(f32[8,16,64]{2,0,1:T(8,128)S(1)} %constant_dynamic-slice_fusion), channel_id=1, replica_groups=mesh['seq'=4,'res'=8] {'seq'}, dimensions={1}, use_global_device_ids=true | all-gather | bytes 163840 | tf_op jit(solution)/shard_map/all_gather | solution.py:96
  125.6 1.3 multiply_reduce_fusion.1
  127.0 2.9 %fusion.4 = f32[8,64,1024]{2,1,0:T(8,128)S(1)} fusion(f32[256,1024]{1,0:T(8,128)S(1)} %copy-done, f32[256]{0:T(256)S(1)} %copy-done.4, f32[8,64]{1,0:T(8,128)S(1)} %rsqrt.28, f32[8,64]{1,0:T(8,128)S(1)} %div.42, f32[8,8,8,256]{3,2,1,0:T(8,128)} %all-to-all-done), kind=kOutput, calls=%fused_computation.11 | convolution fusion | flops 1611005952 | bytes 3675136 | tf_op jit(solution)/shard_map/vmap()/dot_general | solution.py:39
  131.2 2.4 %copy.38 = f32[8,64,256]{1,2,0:T(8,128)} copy(f32[8,64,256]{2,1,0:T(8,128)} %get-tuple-element.2) | data formatting | bytes 1048576 | tf_op jit(solution)/shard_map/vmap()/slice | solution.py:45
  133.6 2.4 %copy.37 = f32[8,64,256]{1,2,0:T(8,128)} copy(f32[8,64,256]{2,1,0:T(8,128)} %get-tuple-element.3) | data formatting | bytes 1048576 | tf_op jit(solution)/shard_map/vmap()/mul | solution.py:42
  136.0 2.4 %copy.36 = f32[8,64,256]{1,2,0:T(8,128)} copy(f32[8,64,256]{2,1,0:T(8,128)} %get-tuple-element.4) | data formatting | bytes 1048576 | tf_op jit(solution)/shard_map/vmap()/slice | solution.py:46
  138.4 5.1 %add_reduce_fusion = (f32[8,8,64]{2,1,0:T(8,128)S(1)}, f32[8,8,64,64]{2,3,1,0:T(8,128)S(1)}) fusion(f32[8,64,64]{1,2,0:T(8,128)S(1)} %copy.43, f32[8,64,8,32]{1,3,2,0:T(8,128)} %bitcast.72, f32[8,64,8,32]{1,3,2,0:T(8,128)} %bitcast.71), kind=kOutput, calls=%fused_computation.4 | convolution fusion | flops 101183488 | bytes 2244608 | tf_op jit(solution)/shard_map/vmap(ihd,jhd->hij)/dot_general | solution.py:48
  144.7 3.3 %fusion = f32[8,8,32,64]{3,2,1,0:T(8,128)} fusion(f32[8,64,8,32]{1,3,2,0:T(8,128)S(1)} %bitcast.78, f32[8,8,64,64]{2,3,1,0:T(8,128)S(1)} %get-tuple-element.10, f32[8,8,64]{2,1,0:T(8,128)S(1)} %fusion.2, f32[8,8,64]{2,1,0:T(8,128)S(1)} %get-tuple-element.9, f32[8,64,64]{1,2,0:T(8,128)S(1)} %copy.43), kind=kOutput, calls=%fused_computation | convolution fusion | flops 101449728 | bytes 2260992 | tf_op jit(solution)/shard_map/vmap(hij,jhd->ihd)/dot_general | solution.py:50
  148.0 2.3 %copy.45 = f32[8,64,256]{2,1,0:T(8,128)} copy(f32[8,64,256]{1,2,0:T(8,128)} %bitcast.79) | data formatting | bytes 1048576 | tf_op jit(solution)/shard_map/vmap()/reshape | solution.py:50
  150.4 2.0 %fusion.3 = f32[1,8,64,256]{3,2,1,0:T(8,128)S(1)} fusion(f32[8,64,256]{2,1,0:T(8,128)} %copy.45, f32[8,64,1024]{2,1,0:T(8,128)S(1)} %fusion.4, f32[256,256]{1,0:T(8,128)} %param.19, f32[8,8,8,256]{3,2,1,0:T(8,128)} %all-to-all-done), kind=kOutput, calls=%fused_computation.7 | convolution fusion | flops 403308544 | bytes 2359296 | tf_op jit(solution)/shard_map/vmap()/dot_general | solution.py:54
  152.6 17.7 %all_to_all.48 = f32[1,8,64,256]{3,1,0,2:T(8,128)S(1)} all-to-all(f32[1,8,64,256]{3,1,0,2:T(8,128)S(1)} %copy.46), channel_id=1, replica_groups=mesh['seq'=4,'res'=8] {'res'}, dimensions={2} | all-to-all | bytes 1048576 | tf_op jit(solution)/shard_map/all_to_all | solution.py:110
  (49 shorter events, 10.0 us)
Async XLA Ops:
  0.6 126.4 %copy-start = (f32[256,1024]{1,0:T(8,128)S(1)}, f32[256,1024]{1,0:T(8,128)}, u32[]{:S(2)}) copy-start(f32[256,1024]{1,0:T(8,128)} %param.18) | copy-start | bytes 3145732
  35.0 22.6 %all-to-all-start.1 = ((f32[4,1,32768]{2,1,0:T(1,128)}), f32[4,1,32768]{2,1,0:T(1,128)S(1)}, u32[]{:S(2)}, u32[]{:S(2)}) async-start(f32[4,1,32768]{2,1,0:T(1,128)} %reshape.99), calls=%async_computation.1 | async-start | bytes 1048576 | tf_op jit(solution)/shard_map/all_to_all | solution.py:82
  57.6 66.7 %all-to-all-start = ((f32[8,8,8,256]{3,2,1,0:T(8,128)}), f32[8,8,8,256]{3,2,1,0:T(8,128)}, u32[]{:S(2)}, u32[]{:S(2)}) async-start(f32[8,8,8,256]{3,2,1,0:T(8,128)} %bitcast), calls=%async_computation | async-start | bytes 1048576 | tf_op jit(solution)/shard_map/all_to_all | solution.py:103
  71.9 1.8 %copy-start.3 = (f32[16,8,128]{2,1,0:T(8,128)S(1)}, f32[16,8,128]{2,1,0:T(8,128)}, u32[]{:S(2)}) copy-start(f32[16,8,128]{2,1,0:T(8,128)} %param.11) | copy-start | bytes 196612
  71.9 3.9 %copy-start.5 = (f32[128,8]{0,1:T(8,128)S(1)}, f32[128,8]{0,1:T(8,128)}, u32[]{:S(2)}) copy-start(f32[128,8]{0,1:T(8,128)} %param.16) | copy-start | bytes 12292
  71.9 3.9 %copy-start.6 = (f32[128]{0:T(128)S(1)}, f32[128]{0:T(128)}, u32[]{:S(2)}) copy-start(f32[128]{0:T(128)} %param.15) | copy-start | bytes 1540
  75.6 54.4 %copy-start.2 = (f32[16,8,128]{2,1,0:T(8,128)}, f32[16,8,128]{2,1,0:T(8,128)S(1)}, u32[]{:S(2)}) copy-start(f32[16,8,128]{2,1,0:T(8,128)S(1)} %get-tuple-element.8) | copy-start | bytes 196612
  75.6 51.4 %copy-start.4 = (f32[256]{0:T(256)S(1)}, f32[256]{0:T(256)}, u32[]{:S(2)}) copy-start(f32[256]{0:T(256)} %param.17) | copy-start | bytes 3076
  76.9 5.5 %collective-permute-start = (f32[8,16,8]{2,0,1:T(8,128)S(1)}, f32[8,16,8]{2,0,1:T(8,128)S(1)}, u32[]{:S(2)}, u32[]{:S(2)}) collective-permute-start(f32[8,16,8]{2,0,1:T(8,128)S(1)} %convolution_bitcast_fusion.1), channel_id=1, source_target_pairs={{0,1},{1,2},{2,3},{3,4},{4,5},{5,6},{6,7},{7,0},{8,9},{9,10},{10,1... | collective-permute-start | bytes 12296 | tf_op jit(solution)/shard_map/ppermute | solution.py:16
  82.4 5.5 %collective-permute-start.1 = (f32[8,16,8]{2,0,1:T(8,128)S(1)}, f32[8,16,8]{2,0,1:T(8,128)S(1)}, u32[]{:S(2)}, u32[]{:S(2)}) collective-permute-start(f32[8,16,8]{2,0,1:T(8,128)S(1)} %collective-permute-done), channel_id=1, source_target_pairs={{0,1},{1,2},{2,3},{3,4},{4,5},{5,6},{6,7},{7,0},{8,9},{9,10},{10,1... | collective-permute-start | bytes 12296 | tf_op jit(solution)/shard_map/ppermute | solution.py:16
  87.9 5.5 %collective-permute-start.2 = (f32[8,16,8]{2,0,1:T(8,128)S(1)}, f32[8,16,8]{2,0,1:T(8,128)S(1)}, u32[]{:S(2)}, u32[]{:S(2)}) collective-permute-start(f32[8,16,8]{2,0,1:T(8,128)S(1)} %collective-permute-done.1), channel_id=1, source_target_pairs={{0,1},{1,2},{2,3},{3,4},{4,5},{5,6},{6,7},{7,0},{8,9},{9,10},{10,1... | collective-permute-start | bytes 12296 | tf_op jit(solution)/shard_map/ppermute | solution.py:16
  93.4 5.5 %collective-permute-start.3 = (f32[8,16,8]{2,0,1:T(8,128)S(1)}, f32[8,16,8]{2,0,1:T(8,128)S(1)}, u32[]{:S(2)}, u32[]{:S(2)}) collective-permute-start(f32[8,16,8]{2,0,1:T(8,128)S(1)} %collective-permute-done.2), channel_id=1, source_target_pairs={{0,1},{1,2},{2,3},{3,4},{4,5},{5,6},{6,7},{7,0},{8,9},{9,10},{10,1... | collective-permute-start | bytes 12296 | tf_op jit(solution)/shard_map/ppermute | solution.py:16
  98.9 5.5 %collective-permute-start.4 = (f32[8,16,8]{2,0,1:T(8,128)S(1)}, f32[8,16,8]{2,0,1:T(8,128)S(1)}, u32[]{:S(2)}, u32[]{:S(2)}) collective-permute-start(f32[8,16,8]{2,0,1:T(8,128)S(1)} %collective-permute-done.3), channel_id=1, source_target_pairs={{0,1},{1,2},{2,3},{3,4},{4,5},{5,6},{6,7},{7,0},{8,9},{9,10},{10,1... | collective-permute-start | bytes 12296 | tf_op jit(solution)/shard_map/ppermute | solution.py:16
  104.4 5.5 %collective-permute-start.5 = (f32[8,16,8]{2,0,1:T(8,128)S(1)}, f32[8,16,8]{2,0,1:T(8,128)S(1)}, u32[]{:S(2)}, u32[]{:S(2)}) collective-permute-start(f32[8,16,8]{2,0,1:T(8,128)S(1)} %collective-permute-done.4), channel_id=1, source_target_pairs={{0,1},{1,2},{2,3},{3,4},{4,5},{5,6},{6,7},{7,0},{8,9},{9,10},{10,1... | collective-permute-start | bytes 12296 | tf_op jit(solution)/shard_map/ppermute | solution.py:16
  109.9 5.5 %collective-permute-start.6 = (f32[8,16,8]{2,0,1:T(8,128)S(1)}, f32[8,16,8]{2,0,1:T(8,128)S(1)}, u32[]{:S(2)}, u32[]{:S(2)}) collective-permute-start(f32[8,16,8]{2,0,1:T(8,128)S(1)} %collective-permute-done.5), channel_id=1, source_target_pairs={{0,1},{1,2},{2,3},{3,4},{4,5},{5,6},{6,7},{7,0},{8,9},{9,10},{10,1... | collective-permute-start | bytes 12296 | tf_op jit(solution)/shard_map/ppermute | solution.py:16
  143.5 1.2 copy-start.1
